TPU v7x, 32 devices: a whole 2x2x4 slice. The times are simulated.
32 devices in a mesh: band: 8 (over y, x, core), bus: 4 (over z).
Axes of the slice: x: 2, y: 2, z: 4, core: 2. Of those that a mesh axis runs over, the one named last changes fastest.
Arguments:
- dispatch0: float32 [64, 5120], P(None, ('band', 'bus')), may hold values from 0 to 1
- cost_lin: float32 [5120], P(('band', 'bus')), may hold values from -1 to 1
- cost_quad: float32 [5120], P(('band', 'bus')), may hold values from 0.5 to 4
- gen_max: float32 [5120], P(('band', 'bus')), may hold values from 0.5 to 2
- bus_map: int32 [5120], P(('band', 'bus')), may hold values from 0 to 98303, as said below
- demand: float32 [64, 4, 24576], P(None, 'bus', 'band'), may hold values from -6 to 6
- ptdf: float32 [2048, 98304], P('band', 'bus'), may hold values from -0.01953125 to 0.01953125
- line_price0: float32 [64, 2048], P(None, 'band'), may hold values from -3 to 3
- flow_max: float32 [2048], P('band'), may hold values from 0.3 to 3
Outputs:
- dispatch: float32 [64, 5120], P(None, ('band', 'bus'))
- line_price: float32 [64, 2048], P(None, 'band')
Inputs may be any that keep to these rules, and one draw needn't show every extreme that they name: `bus_map`: call bus 24576 * j + 3072 * i + k with 0 <= k < 3072 a bus of sub-block (i, j). Among the 160 generators of one aligned block (generators 160 * d to 160 * d + 159), at most 6 are sited in one sub-block, and one sub-block holds exactly 6 generators of every block.
All inputs are finite; a program needn't handle non-finite values.
Results may differ from a plain program's by a relative error of at most 0.0003.
Values sent between devices are 32-bit elements; how exact they have to be, the bound alone decides.
A program may use at most 128 MiB of HBM per device.

v0:
```python
import jax
import jax.numpy as jnp
from jax import lax
from jax.sharding import PartitionSpec as P

ITERS = 2
primal_step = 0.5
dual_step = 1.0


def owner_slots(bus_map, bus_width, sub_width, bus_count, slot_cap):
    block = bus_map // bus_width
    within = bus_map % bus_width
    owner = within // sub_width * bus_count + block
    local = within % sub_width
    same = owner[:, None] == owner[None, :]
    earlier = lax.broadcasted_iota(jnp.int32, same.shape, 0) > lax.broadcasted_iota(
        jnp.int32, same.shape, 1
    )
    rank = jnp.sum((same & earlier).astype(jnp.int32), axis=1)
    return (owner * slot_cap + rank, local)


def pack_rows(values, target, total):
    return jnp.zeros((total, values.shape[1]), values.dtype).at[target].set(values)


def on_device(
    dispatch0, cost_lin, cost_quad, gen_max, bus_map, demand, ptdf, line_price0, flow_max
):
    band_count = lax.axis_size("band")
    bus_count = lax.axis_size("bus")
    owner_count = band_count * bus_count
    gen_count = bus_map.shape[0]
    slot_cap = (gen_count + owner_count - 1) // owner_count + 1
    total = owner_count * slot_cap
    scenarios = dispatch0.shape[0]
    sub_width = demand.shape[2]
    bus_width = ptdf.shape[1]
    target, local = owner_slots(bus_map, bus_width, sub_width, bus_count, slot_cap)
    site_code = (local + 1).astype(jnp.float32)
    load = demand[:, 0, :]
    line_price = line_price0
    dispatch = dispatch0
    code_out = pack_rows(site_code[:, None], target, total).reshape(owner_count, slot_cap)
    column_ids = None
    for iteration in range(ITERS):
        sent = pack_rows(dispatch.T, target, total).reshape(owner_count, slot_cap * scenarios)
        arrived, codes = (
            lax.all_to_all(sent, ("band", "bus"), split_axis=0, concat_axis=0, tiled=True),
            lax.all_to_all(code_out, ("band", "bus"), split_axis=0, concat_axis=0, tiled=True),
        )
        slot_local = jnp.maximum(codes.reshape(total) - 1.0, 0.0).astype(jnp.int32)
        spread = (
            jnp.zeros((sub_width, scenarios), jnp.float32)
            .at[slot_local]
            .add(arrived.reshape(total, scenarios))
        )
        injection = spread.T - load
        flow = lax.psum(
            lax.dot_general(
                lax.all_gather(injection, "band", axis=1, tiled=True),
                ptdf,
                (((1,), (1,)), ((), ())),
                precision=lax.Precision.HIGHEST,
                preferred_element_type=jnp.float32,
            ),
            "bus",
        )
        bound = dual_step * flow_max
        trial = line_price + dual_step * flow
        price_next = trial - jnp.clip(trial, -bound, bound)
        line_price, reflected = (price_next, 2.0 * price_next - line_price)
        if iteration == 0:
            gathered = lax.all_gather(slot_local, "band", axis=0, tiled=True)
            position = lax.broadcasted_iota(jnp.int32, gathered.shape, 0)
            column_ids = position // total * sub_width + gathered
        rows_columns = jnp.take(ptdf, column_ids, axis=1)
        slot_price = lax.psum_scatter(
            lax.dot_general(
                rows_columns,
                reflected,
                (((0,), (1,)), ((), ())),
                precision=lax.Precision.HIGHEST,
                preferred_element_type=jnp.float32,
            ),
            "band",
            scatter_dimension=0,
            tiled=True,
        )
        answer = slot_price.reshape(owner_count, slot_cap * scenarios)
        back = lax.all_to_all(answer, ("band", "bus"), split_axis=0, concat_axis=0, tiled=True)
        unit_price = back.reshape(total, scenarios)[target].T
        dispatch = jnp.clip(
            (dispatch - primal_step * (cost_lin[None, :] + unit_price))
            / (1.0 + primal_step * cost_quad[None, :]),
            0.0,
            gen_max[None, :],
        )
    return (dispatch, line_price)


def solution(mesh):
    in_specs = (
        P(None, ("band", "bus")),
        P(("band", "bus")),
        P(("band", "bus")),
        P(("band", "bus")),
        P(("band", "bus")),
        P(None, "bus", "band"),
        P("band", "bus"),
        P(None, "band"),
        P("band"),
    )
    out_specs = (P(None, ("band", "bus")), P(None, "band"))
    return jax.shard_map(
        on_device, mesh=mesh, in_specs=in_specs, out_specs=out_specs, check_vma=False
    )
```

profile of v0, /device:TPU:0, one launch (start us, length us, event | category | flops | bytes accessed | tf_op | source)
XLA Modules:
  0.0 428.0 jit_solution(5949450486282528453)
XLA Ops:
  8.1 1.1 scatter_custom_fusion
  9.9 7.3 %all-to-all-start = ((f32[32,1,6]{2,1,0:T(1,128)}), f32[32,1,6]{2,1,0:T(1,128)S(1)}, u32[]{:S(2)}, u32[]{:S(2)}) async-start(f32[32,1,6]{2,1,0:T(1,128)} %bitcast), calls=%async_computation | async-start | bytes 32768 | tf_op jit(solution)/shard_map/all_to_all | solution.py:51
  17.3 2.3 copy.38
  19.7 1.0 scatter_custom_fusion.1
  21.4 3.0 all-to-all-done
  24.4 2.9 all-to-all-start.1
  27.5 7.2 %all-to-all-done.1 = f32[32,1,384]{2,1,0:T(1,128)S(1)} async-done(((f32[32,1,384]{2,1,0:T(1,128)}), f32[32,1,384]{2,1,0:T(1,128)S(1)}, u32[]{:S(2)}, u32[]{:S(2)}) %all-to-all-start.1) | async-done | bytes 49184 | tf_op jit(solution)/shard_map/all_to_all | solution.py:50
  34.9 1.6 scatter_custom_fusion.2
  36.5 1.3 bitcast_subtract_fusion.1
  37.9 25.0 %copy.35 = f32[256,24576]{0,1:T(8,128)} copy(f32[256,24576]{1,0:T(8,128)} %param.17) | data formatting | bytes 50331648 | tf_op args[6]
  64.6 6.6 %all-reduce = s32[1536]{0:T(1024)S(1)} all-reduce(s32[1536]{0:T(1024)S(1)} %dynamic-update-slice), channel_id=1, replica_groups=mesh['band'=8,'bus'=4] {'band'}, use_global_device_ids=true, to_apply=%add | all-reduce | flops 1536 | bytes 12288
  71.2 35.3 %all-gather.3.cloned.1.call-done = f32[64,24576]{0,1:T(8,128)} async-done(((f32[64,3072]{0,1:T(8,128)}), f32[64,24576]{0,1:T(8,128)}) %all-gather.3.cloned.1.call-update) | async-done | bytes 6291472 | tf_op jit(solution)/shard_map/all_gather | solution.py:62
  106.5 27.7 %fusion.48 = f32[64,256]{1,0:T(8,128)} fusion(f32[64,24576]{0,1:T(8,128)} %all-gather.3.cloned.1.call-done, f32[256,24576]{1,0:T(8,128)} %param.17), kind=kOutput, calls=%fused_computation.81 | convolution fusion | flops 4831838208 | bytes 31522816 | tf_op jit(solution)/shard_map/dot_general | solution.py:61
  134.5 11.9 %gather_fusion.2 = f32[1536,256]{1,0:T(8,128)S(1)} fusion(f32[256,24576]{0,1:T(8,128)} %copy.35, s32[2048]{0:T(1024)S(1)} %pad_clamp_fusion), kind=kCustom, calls=%fused_computation.clone | custom fusion | bytes 3151872 | tf_op jit(solution)/shard_map/jit(_take)/gather | solution.py:78
  146.4 22.2 %all-reduce.4.cloned.1.call-done = f32[64,256]{1,0:T(8,128)} async-done(((f32[64,256]{1,0:T(8,128)}), f32[64,256]{1,0:T(8,128)}) %all-reduce.4.cloned.1.call-update) | async-done | bytes 65552 | tf_op jit(solution)/shard_map/psum | solution.py:60
  168.6 3.2 fusion.2
  171.9 34.7 %reduce-scatter.7.cloned.1.call-done = f32[192,64]{1,0:T(8,128)} async-done(((f32[1536,64]{1,0:T(8,128)}), f32[192,64]{1,0:T(8,128)}) %reduce-scatter.7.cloned.1.call-update) | async-done | bytes 49168 | tf_op jit(solution)/shard_map/reduce_scatter | solution.py:79
  206.6 1.6 all_to_all.42
  208.2 4.6 %all-to-all-start.2 = ((f32[32,1,384]{2,1,0:T(1,128)}), f32[32,1,384]{2,1,0:T(1,128)S(1)}, u32[]{:S(2)}, u32[]{:S(2)}) async-start(f32[32,1,384]{2,1,0:T(1,128)} %all_to_all.42), calls=%async_computation.2 | async-start | bytes 98304 | tf_op jit(solution)/shard_map/all_to_all | solution.py:92
  212.9 7.3 %all-to-all-done.2 = f32[32,1,384]{2,1,0:T(1,128)S(1)} async-done(((f32[32,1,384]{2,1,0:T(1,128)}), f32[32,1,384]{2,1,0:T(1,128)S(1)}, u32[]{:S(2)}, u32[]{:S(2)}) %all-to-all-start.2) | async-done | bytes 49184 | tf_op jit(solution)/shard_map/all_to_all | solution.py:92
  221.1 1.1 scatter_custom_fusion.3
  222.3 9.1 %all_to_all.50 = f32[32,1,384]{2,1,0:T(1,128)S(1)} all-to-all(f32[32,1,384]{2,1,0:T(1,128)S(1)} %all_to_all.43), channel_id=1, replica_groups=mesh['band'=8,'bus'=4] {'band','bus'}, dimensions={0} | all-to-all | bytes 98304 | tf_op jit(solution)/shard_map/all_to_all | solution.py:50
  232.2 2.8 scatter_custom_fusion.4
  235.1 2.8 bitcast_subtract_fusion
  237.9 68.5 %all-gather.5.cloned.1.call-done = f32[64,24576]{0,1:T(8,128)} async-done(((f32[64,3072]{0,1:T(8,128)}), f32[64,24576]{0,1:T(8,128)}) %all-gather.5.cloned.1.call-update) | async-done | bytes 6291472 | tf_op jit(solution)/shard_map/all_gather | solution.py:62
  306.4 27.7 %fusion.49 = f32[64,256]{1,0:T(8,128)} fusion(f32[64,24576]{0,1:T(8,128)} %all-gather.5.cloned.1.call-done, f32[256,24576]{1,0:T(8,128)} %param.17), kind=kOutput, calls=%fused_computation.82 | convolution fusion | flops 4831838208 | bytes 31522816 | tf_op jit(solution)/shard_map/dot_general | solution.py:61
  334.2 34.4 %all-reduce.6.cloned.1.call-done = f32[64,256]{1,0:T(8,128)} async-done(((f32[64,256]{1,0:T(8,128)}), f32[64,256]{1,0:T(8,128)}) %all-reduce.6.cloned.1.call-update) | async-done | bytes 65552 | tf_op jit(solution)/shard_map/psum | solution.py:60
  368.6 0.9 minimum_subtract_fusion
  369.5 2.3 fusion
  371.8 34.8 %reduce-scatter.9.cloned.1.call-done = f32[192,64]{1,0:T(8,128)} async-done(((f32[1536,64]{1,0:T(8,128)}), f32[192,64]{1,0:T(8,128)}) %reduce-scatter.9.cloned.1.call-update) | async-done | bytes 49168 | tf_op jit(solution)/shard_map/reduce_scatter | solution.py:79
  406.6 1.0 all_to_all.44
  407.6 11.8 %all_to_all.51 = f32[32,1,384]{2,1,0:T(1,128)S(1)} all-to-all(f32[32,1,384]{2,1,0:T(1,128)S(1)} %all_to_all.44), channel_id=1, replica_groups=mesh['band'=8,'bus'=4] {'band','bus'}, dimensions={0} | all-to-all | bytes 98304 | tf_op jit(solution)/shard_map/all_to_all | solution.py:92
  (65 shorter events, 8.1 us)
Async XLA Ops:
  7.2 12.4 %copy-start.2 = (f32[64,160]{1,0:T(8,128)S(1)}, f32[64,160]{1,0:T(8,128)}, u32[]{:S(2)}) copy-start(f32[64,160]{1,0:T(8,128)} %param.11) | copy-start | bytes 122884
  9.9 14.5 %all-to-all-start = ((f32[32,1,6]{2,1,0:T(1,128)}), f32[32,1,6]{2,1,0:T(1,128)S(1)}, u32[]{:S(2)}, u32[]{:S(2)}) async-start(f32[32,1,6]{2,1,0:T(1,128)} %bitcast), calls=%async_computation | async-start | bytes 32768 | tf_op jit(solution)/shard_map/all_to_all | solution.py:51
  24.4 10.3 %all-to-all-start.1 = ((f32[32,1,384]{2,1,0:T(1,128)}), f32[32,1,384]{2,1,0:T(1,128)S(1)}, u32[]{:S(2)}, u32[]{:S(2)}) async-start(f32[32,1,384]{2,1,0:T(1,128)} %all_to_all.41), calls=%async_computation.1 | async-start | bytes 98304 | tf_op jit(solution)/shard_map/all_to_all | solution.py:50
  27.3 79.2 %all-gather.3.cloned.1.call-start = ((), (), s32[]{:S(2)}) async-start(), calls=%async_computation.7 | async-start | bytes 14155776 | tf_op jit(solution)/shard_map/all_gather | solution.py:62
  27.5 10.3 %copy-start.8 = (s32[192,1]{0,1:T(1,128)}, s32[192,1]{0,1:T(1,128)S(1)}, u32[]{:S(2)}) copy-start(s32[192,1]{0,1:T(1,128)S(1)} %compare_select_fusion.1) | copy-start | bytes 2308
  37.8 130.8 %all-reduce.4.cloned.1.call-start = ((), (), s32[]{:S(2)}) async-start(), calls=%async_computation.8 | async-start | bytes 131072 | tf_op jit(solution)/shard_map/psum | solution.py:60
  37.9 25.0 %copy-start.4 = (f32[256]{0:T(256)S(1)}, f32[256]{0:T(256)}, u32[]{:S(2)}) copy-start(f32[256]{0:T(256)} %param.19) | copy-start | bytes 3076
  37.9 25.0 %copy-start.9 = (u32[32]{0:T(128)S(1)}, u32[32]{0:T(128)}, u32[]{:S(2)}) copy-start(u32[32]{0:T(128)} %constant.80) | copy-start | bytes 388
  134.2 72.3 %reduce-scatter.7.cloned.1.call-start = ((), (), s32[]{:S(2)}) async-start(), calls=%async_computation.11 | async-start | bytes 884736 | tf_op jit(solution)/shard_map/reduce_scatter | solution.py:79
  134.5 34.1 %copy-start = (f32[64,256]{1,0:T(8,128)S(1)}, f32[64,256]{1,0:T(8,128)}, u32[]{:S(2)}) copy-start(f32[64,256]{1,0:T(8,128)} %param.18) | copy-start | bytes 196612
  168.6 3.3 copy-start.7
  171.8 49.3 %copy-start.5 = (f32[160]{0:T(256)S(1)}, f32[160]{0:T(256)}, u32[]{:S(2)}) copy-start(f32[160]{0:T(256)} %param.12) | copy-start | bytes 1924
  171.8 49.3 %copy-start.6 = (f32[160]{0:T(256)S(1)}, f32[160]{0:T(256)}, u32[]{:S(2)}) copy-start(f32[160]{0:T(256)} %param.14) | copy-start | bytes 1924
  208.2 12.0 %all-to-all-start.2 = ((f32[32,1,384]{2,1,0:T(1,128)}), f32[32,1,384]{2,1,0:T(1,128)S(1)}, u32[]{:S(2)}, u32[]{:S(2)}) async-start(f32[32,1,384]{2,1,0:T(1,128)} %all_to_all.42), calls=%async_computation.2 | async-start | bytes 98304 | tf_op jit(solution)/shard_map/all_to_all | solution.py:92
  212.8 93.6 %all-gather.5.cloned.1.call-start = ((), (), s32[]{:S(2)}) async-start(), calls=%async_computation.9 | async-start | bytes 14155776 | tf_op jit(solution)/shard_map/all_gather | solution.py:62
  237.9 130.8 %copy-start.1 = (f32[64,256]{1,0:T(8,128)S(1)}, f32[64,256]{1,0:T(8,128)}, u32[]{:S(2)}) copy-start(f32[64,256]{1,0:T(8,128)} %all-reduce.4.cloned.1.call-done) | copy-start | bytes 196612
  237.9 130.7 %all-reduce.6.cloned.1.call-start = ((), (), s32[]{:S(2)}) async-start(), calls=%async_computation.10 | async-start | bytes 131072 | tf_op jit(solution)/shard_map/psum | solution.py:60
  334.1 72.5 %reduce-scatter.9.cloned.1.call-start = ((), (), s32[]{:S(2)}) async-start(), calls=%async_computation.12 | async-start | bytes 884736 | tf_op jit(solution)/shard_map/reduce_scatter | solution.py:79
  369.5 2.4 copy-start.3
Sparse Core Ops, SparseCore 0:
  37.9 68.5 all-gather.2
  134.3 34.2 all-reduce.3
  171.9 34.6 reduce-scatter.6
  238.0 68.4 all-gather.4
  334.3 34.2 all-reduce.5
  371.9 34.6 reduce-scatter.8
where the time goes:
time: 429 us; the launch traced here: 428 us
  waiting for transfers between devices  247 us (58%)
  matrix products  60.9 us (14%)
  local copies, waits for them, and re-layouts  49.7 us (12%)
  blocking collectives  27.5 us (6%)
  starting transfers between devices  15.3 us (4%)
  between operations  15.1 us (4%)
  other arithmetic  12.1 us (3%)
    all_gather x2, waiting for transfers between devices, on_device(): lax.all_gather(injection, 'band', axis=1, tiled=True)  104 us
    reduce_scatter x2, waiting for transfers between devices, on_device(): lax.psum_scatter(lax.dot_general(rows_columns, reflected, (((0,), (1,)),...  69.5 us
    psum x2, waiting for transfers between devices, on_device(): lax.psum(lax.dot_general(lax.all_gather(injection, 'band', axis=1, tiled=...  56.6 us
    dot_general x2, matrix products, on_device(): lax.dot_general(lax.all_gather(injection, 'band', axis=1, tiled=True), pt...  55.4 us
    unnamed x26, local copies, waits for them, and re-layouts  29 us
    gather x1, local copies, waits for them, and re-layouts, on_device(): rows_columns = jnp.take(ptdf, column_ids, axis=1)  11.9 us
    all_to_all x1, blocking collectives, on_device(): lax.all_to_all(answer, ('band', 'bus'), split_axis=0, concat_axis=0, tile...  11.8 us
    all_to_all x1, blocking collectives, on_device(): lax.all_to_all(sent, ('band', 'bus'), split_axis=0, concat_axis=0, tiled=...  9.09 us
  transfers between devices with their start and end apart: 9, of which 9 were waited for; matrix products, arithmetic and copies ran while one was open for 10% of the time, Pallas kernels for 0%

commit v1 on v0

--- a/solution.py
+++ b/solution.py
@@ -6,6 +6,28 @@
 ITERS = 2
 primal_step = 0.5
 dual_step = 1.0
+
+
+def joined_along(blocks, dim):
+    shape = list(blocks.shape[1:])
+    shape[dim] *= blocks.shape[0]
+    return jnp.moveaxis(blocks, 0, dim).reshape(shape)
+
+
+def grow_blocks(array, axis):
+    size = lax.axis_size(axis)
+    pieces = array[None]
+    for level in range(size.bit_length() - 1):
+        distance = 1 << level
+        other = lax.ppermute(pieces, axis, [(i, i ^ distance) for i in range(size)])
+        both = jnp.stack([pieces, other])
+        upper = lax.axis_index(axis) >> level & 1
+        pieces = jnp.where(upper == 0, both, both[::-1]).reshape(-1, *array.shape)
+    return pieces
+
+
+def collect(x, axis, dim):
+    return joined_along(grow_blocks(x, axis), dim)
 
 
 def owner_slots(bus_map, bus_width, sub_width, bus_count, slot_cap):
@@ -59,7 +81,7 @@
         injection = spread.T - load
         flow = lax.psum(
             lax.dot_general(
-                lax.all_gather(injection, "band", axis=1, tiled=True),
+                collect(injection, "band", 1),
                 ptdf,
                 (((1,), (1,)), ((), ())),
                 precision=lax.Precision.HIGHEST,

time: 429 us -> 571 us (1.33)
  local copies, waits for them, and re-layouts: 49.7 us -> 94.5 us
  blocking collectives: 27.5 us -> 63.6 us
  other arithmetic: 12.1 us -> 43.4 us
  waiting for transfers between devices: 247 us -> 275 us
    ppermute x0 -> x6, waiting for transfers between devices: none -> 139 us  [grow_blocks(): other = lax.ppermute(pieces, axis, [(i, i ^ distance) for i in range(size)])]
    all_gather x2 -> x0, waiting for transfers between devices: 104 us -> none  [on_device(): lax.all_gather(injection, 'band', axis=1, tiled=True)]
    unnamed x1, blocking collectives: 6.56 us -> 42.6 us
    another operation x0 -> x10, other arithmetic: none -> 27.5 us  [grow_blocks(): both = jnp.stack([pieces, other])]
    reshape x0 -> x4, local copies, waits for them, and re-layouts: none -> 16.9 us  [grow_blocks(): pieces = jnp.where(upper == 0, both, both[::-1]).reshape(-1, *array.shape)]
    another operation x0 -> x2, local copies, waits for them, and re-layouts: none -> 12.2 us  [grow_blocks(): both = jnp.stack([pieces, other])]
    ppermute x0 -> x4, local copies, waits for them, and re-layouts: none -> 9.81 us  [grow_blocks(): other = lax.ppermute(pieces, axis, [(i, i ^ distance) for i in range(size)])]
    select_n x0 -> x4, other arithmetic: none -> 7.89 us  [grow_blocks(): pieces = jnp.where(upper == 0, both, both[::-1]).reshape(-1, *array.shape)]
  transfers between devices with their start and end apart: 9 -> 13, of which waited for: 9 -> 12; matrix products, arithmetic and copies ran while one was open for 10% -> 10% of each run, Pallas kernels for 0% -> 0%
where the time goes in v1:
time: 571 us; the launch traced here: 570 us
  waiting for transfers between devices  275 us (48%)
  local copies, waits for them, and re-layouts  94.5 us (17%)
  blocking collectives  63.6 us (11%)
  matrix products  59.3 us (10%)
  other arithmetic  43.4 us (8%)
  starting transfers between devices  18.7 us (3%)
  between operations  14.9 us (3%)
    ppermute x6, waiting for transfers between devices, grow_blocks(): other = lax.ppermute(pieces, axis, [(i, i ^ distance) for i in range(size)])  139 us
    reduce_scatter x2, waiting for transfers between devices, on_device(): lax.psum_scatter(lax.dot_general(rows_columns, reflected, (((0,), (1,)),...  69.4 us
    dot_general x2, matrix products, on_device(): lax.dot_general(collect(injection, 'band', 1), ptdf, (((1,), (1,)), ((),...  53.8 us
    psum x2, waiting for transfers between devices, on_device(): lax.psum(lax.dot_general(collect(injection, 'band', 1), ptdf, (((1,), (1,...  49.9 us
    unnamed x1, blocking collectives  42.6 us
    unnamed x28, local copies, waits for them, and re-layouts  30.2 us
    another operation x10, other arithmetic, grow_blocks(): both = jnp.stack([pieces, other])  27.5 us
    reshape x4, local copies, waits for them, and re-layouts, grow_blocks(): pieces = jnp.where(upper == 0, both, both[::-1]).reshape(-1, *array.shape)  16.9 us
  transfers between devices with their start and end apart: 13, of which 12 were waited for; matrix products, arithmetic and copies ran while one was open for 10% of the time, Pallas kernels for 0%

profile of v1, /device:TPU:0, one launch (start us, length us, event | category | flops | bytes accessed | tf_op | source)
XLA Modules:
  0.0 569.7 jit_solution(786574872112724597)
XLA Ops:
  9.9 7.3 %all-to-all-start = ((f32[32,1,6]{2,1,0:T(1,128)}), f32[32,1,6]{2,1,0:T(1,128)S(1)}, u32[]{:S(2)}, u32[]{:S(2)}) async-start(f32[32,1,6]{2,1,0:T(1,128)} %bitcast), calls=%async_computation | async-start | bytes 32768 | tf_op jit(solution)/shard_map/all_to_all | solution.py:73
  24.3 3.7 all-to-all-start.1
  28.3 7.2 %all-to-all-done.1 = f32[32,1,384]{2,1,0:T(1,128)S(1)} async-done(((f32[32,1,384]{2,1,0:T(1,128)}), f32[32,1,384]{2,1,0:T(1,128)S(1)}, u32[]{:S(2)}, u32[]{:S(2)}) %all-to-all-start.1) | async-done | bytes 49184 | tf_op jit(solution)/shard_map/all_to_all | solution.py:72
  52.8 35.9 %collective-permute-done.1 = f32[2,64,3072]{2,1,0:T(8,128)} collective-permute-done((f32[2,64,3072]{2,1,0:T(8,128)S(1)}, f32[2,64,3072]{2,1,0:T(8,128)}, u32[]{:S(2)}, u32[]{:S(2)}) %collective-permute-start.1) | collective-permute-done | bytes 1572896 | tf_op jit(solution)/shard_map/ppermute | solution.py:22
  88.8 3.3 copy.64
  92.1 3.3 pad_maximum_fusion
  95.3 3.1 reverse_select_fusion.3
  98.4 6.1 %copy.65 = f32[4,64,3072]{2,1,0:T(8,128)} copy(f32[4,64,3072]{1,2,0:T(8,128)} %bitcast.107) | data formatting | bytes 6291456 | tf_op jit(solution)/shard_map/reshape | solution.py:25
  105.2 24.7 %copy.56 = f32[256,24576]{0,1:T(8,128)} copy(f32[256,24576]{1,0:T(8,128)} %param.17) | data formatting | bytes 50331648 | tf_op args[6]
  131.6 42.6 %all-reduce = s32[1536]{0:T(1024)S(1)} all-reduce(s32[1536]{0:T(1024)S(1)} %dynamic-update-slice), channel_id=1, replica_groups=mesh['band'=8,'bus'=4] {'band'}, use_global_device_ids=true, to_apply=%add | all-reduce | flops 1536 | bytes 12288
  174.3 6.1 %copy.66 = f32[1,4,64,3072]{3,2,1,0:T(8,128)} copy(f32[1,4,64,3072]{2,3,1,0:T(8,128)} %bitcast.108) | data formatting | bytes 6291456 | tf_op jit(solution)/shard_map/stack;reshape | solution.py:23
  180.4 3.3 pad_maximum_fusion.1
  185.3 26.9 %fusion.56 = f32[64,256]{1,0:T(8,128)} fusion(f32[64,24576]{1,0:T(8,128)S(1)} %bitcast.113, f32[256,24576]{1,0:T(8,128)} %param.17), kind=kOutput, calls=%fused_computation.101 | convolution fusion | flops 4831838208 | bytes 31522816 | tf_op jit(solution)/shard_map/dot_general | solution.py:83
  212.3 11.9 %gather_fusion.2 = f32[1536,256]{1,0:T(8,128)S(1)} fusion(f32[256,24576]{0,1:T(8,128)} %copy.56, s32[2048]{0:T(1024)S(1)} %pad_clamp_fusion), kind=kCustom, calls=%fused_computation.clone | custom fusion | bytes 3151872 | tf_op jit(solution)/shard_map/jit(_take)/gather | solution.py:100
  224.2 19.1 %all-reduce.4.cloned.1.call-done = f32[64,256]{1,0:T(8,128)} async-done(((f32[64,256]{1,0:T(8,128)}), f32[64,256]{1,0:T(8,128)}) %all-reduce.4.cloned.1.call-update) | async-done | bytes 65552 | tf_op jit(solution)/shard_map/psum | solution.py:82
  243.3 3.1 fusion.6
  246.6 34.6 %reduce-scatter.7.cloned.1.call-done = f32[192,64]{1,0:T(8,128)} async-done(((f32[1536,64]{1,0:T(8,128)}), f32[192,64]{1,0:T(8,128)}) %reduce-scatter.7.cloned.1.call-update) | async-done | bytes 49168 | tf_op jit(solution)/shard_map/reduce_scatter | solution.py:101
  282.9 4.6 all-to-all-start.2
  287.5 7.3 %all-to-all-done.2 = f32[32,1,384]{2,1,0:T(1,128)S(1)} async-done(((f32[32,1,384]{2,1,0:T(1,128)}), f32[32,1,384]{2,1,0:T(1,128)S(1)}, u32[]{:S(2)}, u32[]{:S(2)}) %all-to-all-start.2) | async-done | bytes 49184 | tf_op jit(solution)/shard_map/all_to_all | solution.py:114
  297.0 9.1 %all_to_all.50 = f32[32,1,384]{2,1,0:T(1,128)S(1)} all-to-all(f32[32,1,384]{2,1,0:T(1,128)S(1)} %all_to_all.43), channel_id=1, replica_groups=mesh['band'=8,'bus'=4] {'band','bus'}, dimensions={0} | all-to-all | bytes 98304 | tf_op jit(solution)/shard_map/all_to_all | solution.py:72
  309.7 3.3 fusion.21
  326.7 35.9 %collective-permute-done.4 = f32[2,64,3072]{2,1,0:T(8,128)} collective-permute-done((f32[2,64,3072]{2,1,0:T(8,128)S(1)}, f32[2,64,3072]{2,1,0:T(8,128)}, u32[]{:S(2)}, u32[]{:S(2)}) %collective-permute-start.4) | collective-permute-done | bytes 1572896 | tf_op jit(solution)/shard_map/ppermute | solution.py:22
  362.6 3.3 copy.75
  365.9 3.3 pad_maximum_fusion.2
  372.2 6.1 %copy.76 = f32[4,64,3072]{2,1,0:T(8,128)} copy(f32[4,64,3072]{1,2,0:T(8,128)} %bitcast.109) | data formatting | bytes 6291456 | tf_op jit(solution)/shard_map/reshape | solution.py:25
  379.0 6.1 %copy.77 = f32[1,4,64,3072]{3,2,1,0:T(8,128)} copy(f32[1,4,64,3072]{2,3,1,0:T(8,128)} %bitcast.110) | data formatting | bytes 6291456 | tf_op jit(solution)/shard_map/stack;reshape | solution.py:23
  385.1 62.8 %collective-permute-done.5 = f32[4,64,3072]{2,1,0:T(8,128)} collective-permute-done((f32[4,64,3072]{2,1,0:T(8,128)}, f32[4,64,3072]{2,1,0:T(8,128)}, u32[]{:S(2)}, u32[]{:S(2)}) %collective-permute-start.5) | collective-permute-done | bytes 3145760 | tf_op jit(solution)/shard_map/ppermute | solution.py:22
  447.9 3.3 pad_maximum_fusion.3
  452.8 26.9 %fusion.57 = f32[64,256]{1,0:T(8,128)} fusion(f32[64,24576]{1,0:T(8,128)S(1)} %bitcast.114, f32[256,24576]{1,0:T(8,128)} %param.17), kind=kOutput, calls=%fused_computation.102 | convolution fusion | flops 4831838208 | bytes 31522816 | tf_op jit(solution)/shard_map/dot_general | solution.py:83
  479.8 30.8 %all-reduce.6.cloned.1.call-done = f32[64,256]{1,0:T(8,128)} async-done(((f32[64,256]{1,0:T(8,128)}), f32[64,256]{1,0:T(8,128)}) %all-reduce.6.cloned.1.call-update) | async-done | bytes 65552 | tf_op jit(solution)/shard_map/psum | solution.py:82
  513.8 34.8 %reduce-scatter.9.cloned.1.call-done = f32[192,64]{1,0:T(8,128)} async-done(((f32[1536,64]{1,0:T(8,128)}), f32[192,64]{1,0:T(8,128)}) %reduce-scatter.9.cloned.1.call-update) | async-done | bytes 49168 | tf_op jit(solution)/shard_map/reduce_scatter | solution.py:101
  549.6 11.8 %all_to_all.51 = f32[32,1,384]{2,1,0:T(1,128)S(1)} all-to-all(f32[32,1,384]{2,1,0:T(1,128)S(1)} %all_to_all.44), channel_id=1, replica_groups=mesh['band'=8,'bus'=4] {'band','bus'}, dimensions={0} | all-to-all | bytes 98304 | tf_op jit(solution)/shard_map/all_to_all | solution.py:114
  (97 shorter events, 63.1 us)
Async XLA Ops:
  9.9 14.5 %all-to-all-start = ((f32[32,1,6]{2,1,0:T(1,128)}), f32[32,1,6]{2,1,0:T(1,128)S(1)}, u32[]{:S(2)}, u32[]{:S(2)}) async-start(f32[32,1,6]{2,1,0:T(1,128)} %bitcast), calls=%async_computation | async-start | bytes 32768 | tf_op jit(solution)/shard_map/all_to_all | solution.py:73
  24.3 11.1 %all-to-all-start.1 = ((f32[32,1,384]{2,1,0:T(1,128)}), f32[32,1,384]{2,1,0:T(1,128)S(1)}, u32[]{:S(2)}, u32[]{:S(2)}) async-start(f32[32,1,384]{2,1,0:T(1,128)} %all_to_all.41), calls=%async_computation.1 | async-start | bytes 98304 | tf_op jit(solution)/shard_map/all_to_all | solution.py:72
  28.1 215.2 %all-reduce.4.cloned.1.call-start = ((), (), s32[]{:S(2)}) async-start(), calls=%async_computation.7 | async-start | bytes 131072 | tf_op jit(solution)/shard_map/psum | solution.py:82
  28.3 10.9 %copy-start.8 = (s32[192,1]{0,1:T(1,128)}, s32[192,1]{0,1:T(1,128)S(1)}, u32[]{:S(2)}) copy-start(s32[192,1]{0,1:T(1,128)S(1)} %compare_select_fusion.1) | copy-start | bytes 2308
  41.0 2.5 collective-permute-start
  52.1 36.6 %collective-permute-start.1 = (f32[2,64,3072]{2,1,0:T(8,128)S(1)}, f32[2,64,3072]{2,1,0:T(8,128)}, u32[]{:S(2)}, u32[]{:S(2)}) collective-permute-start(f32[2,64,3072]{2,1,0:T(8,128)S(1)} %copy.63), channel_id=1, source_target_pairs={{0,8},{4,12},{8,0},{12,4},{16,24},{20,28},{24,16},{28,20},{1,9},{5... | collective-permute-start | bytes 4718600 | tf_op jit(solution)/shard_map/ppermute | solution.py:22
  104.6 75.8 %collective-permute-start.2 = (f32[4,64,3072]{2,1,0:T(8,128)}, f32[4,64,3072]{2,1,0:T(8,128)}, u32[]{:S(2)}, u32[]{:S(2)}) collective-permute-start(f32[4,64,3072]{2,1,0:T(8,128)} %copy.65), channel_id=1, source_target_pairs={{0,16},{4,20},{8,24},{12,28},{16,0},{20,4},{24,8},{28,12},{1,17},{... | collective-permute-start | bytes 9437192 | tf_op jit(solution)/shard_map/ppermute | solution.py:22
  105.2 24.7 %copy-start.4 = (f32[256]{0:T(256)S(1)}, f32[256]{0:T(256)}, u32[]{:S(2)}) copy-start(f32[256]{0:T(256)} %param.19) | copy-start | bytes 3076
  105.2 24.7 %copy-start.9 = (u32[32]{0:T(128)S(1)}, u32[32]{0:T(128)}, u32[]{:S(2)}) copy-start(u32[32]{0:T(128)} %constant.89) | copy-start | bytes 388
  212.2 69.0 %reduce-scatter.7.cloned.1.call-start = ((), (), s32[]{:S(2)}) async-start(), calls=%async_computation.9 | async-start | bytes 884736 | tf_op jit(solution)/shard_map/reduce_scatter | solution.py:101
  212.3 31.0 %copy-start = (f32[64,256]{1,0:T(8,128)S(1)}, f32[64,256]{1,0:T(8,128)}, u32[]{:S(2)}) copy-start(f32[64,256]{1,0:T(8,128)} %param.18) | copy-start | bytes 196612
  224.2 22.3 %copy-start.2 = (f32[64,160]{1,0:T(8,128)S(1)}, f32[64,160]{1,0:T(8,128)}, u32[]{:S(2)}) copy-start(f32[64,160]{1,0:T(8,128)} %param.11) | copy-start | bytes 122884
  224.2 22.4 %copy-start.7 = (f32[160]{0:T(256)S(1)}, f32[160]{0:T(256)}, u32[]{:S(2)}) copy-start(f32[160]{0:T(256)} %param.13) | copy-start | bytes 1924
  224.2 71.6 %copy-start.5 = (f32[160]{0:T(256)S(1)}, f32[160]{0:T(256)}, u32[]{:S(2)}) copy-start(f32[160]{0:T(256)} %param.12) | copy-start | bytes 1924
  224.2 71.5 %copy-start.6 = (f32[160]{0:T(256)S(1)}, f32[160]{0:T(256)}, u32[]{:S(2)}) copy-start(f32[160]{0:T(256)} %param.14) | copy-start | bytes 1924
  282.9 12.0 %all-to-all-start.2 = ((f32[32,1,384]{2,1,0:T(1,128)}), f32[32,1,384]{2,1,0:T(1,128)S(1)}, u32[]{:S(2)}, u32[]{:S(2)}) async-start(f32[32,1,384]{2,1,0:T(1,128)} %all_to_all.42), calls=%async_computation.2 | async-start | bytes 98304 | tf_op jit(solution)/shard_map/all_to_all | solution.py:114
  287.5 223.1 %all-reduce.6.cloned.1.call-start = ((), (), s32[]{:S(2)}) async-start(), calls=%async_computation.8 | async-start | bytes 131072 | tf_op jit(solution)/shard_map/psum | solution.py:82
  314.8 2.5 collective-permute-start.3
  326.0 36.6 %collective-permute-start.4 = (f32[2,64,3072]{2,1,0:T(8,128)S(1)}, f32[2,64,3072]{2,1,0:T(8,128)}, u32[]{:S(2)}, u32[]{:S(2)}) collective-permute-start(f32[2,64,3072]{2,1,0:T(8,128)S(1)} %copy.74), channel_id=1, source_target_pairs={{0,8},{4,12},{8,0},{12,4},{16,24},{20,28},{24,16},{28,20},{1,9},{5... | collective-permute-start | bytes 4718600 | tf_op jit(solution)/shard_map/ppermute | solution.py:22
  378.3 69.6 %collective-permute-start.5 = (f32[4,64,3072]{2,1,0:T(8,128)}, f32[4,64,3072]{2,1,0:T(8,128)}, u32[]{:S(2)}, u32[]{:S(2)}) collective-permute-start(f32[4,64,3072]{2,1,0:T(8,128)} %copy.76), channel_id=1, source_target_pairs={{0,16},{4,20},{8,24},{12,28},{16,0},{20,4},{24,8},{28,12},{1,17},{... | collective-permute-start | bytes 9437192 | tf_op jit(solution)/shard_map/ppermute | solution.py:22
  452.8 57.8 %copy-start.1 = (f32[64,256]{1,0:T(8,128)S(1)}, f32[64,256]{1,0:T(8,128)}, u32[]{:S(2)}) copy-start(f32[64,256]{1,0:T(8,128)} %all-reduce.4.cloned.1.call-done) | copy-start | bytes 196612
  479.7 68.9 %reduce-scatter.9.cloned.1.call-start = ((), (), s32[]{:S(2)}) async-start(), calls=%async_computation.10 | async-start | bytes 884736 | tf_op jit(solution)/shard_map/reduce_scatter | solution.py:101
  511.5 51.7 %copy-start.3 = (f32[64,256]{1,0:T(8,128)}, f32[64,256]{1,0:T(8,128)S(1)}, u32[]{:S(2)}) copy-start(f32[64,256]{1,0:T(8,128)S(1)} %minimum_subtract_fusion) | copy-start | bytes 196612
Sparse Core Ops, SparseCore 0:
  212.3 30.9 all-reduce.3
  246.6 34.6 reduce-scatter.6
  479.9 30.6 all-reduce.5
  514.0 34.6 reduce-scatter.8
